TPU v7x, 32 devices: a whole 2x2x4 slice. The times are simulated.
32 devices in a mesh: ctx: 2 (over x), tp: 4 (over y, core), dp: 4 (over z).
Axes of the slice: x: 2, y: 2, z: 4, core: 2. Of those that a mesh axis runs over, the one named last changes fastest.
Arguments:
- byte_embed: bfloat16 [8192, 1024], P(('dp', 'ctx', 'tp')), parts along dimension 0, may hold values from -6 to 6
- patch_start: int32 [8192], P(('dp', 'ctx', 'tp')), parts along dimension 0, may hold values from 0 to 1, as said below
- enc_gain: float32 [1024], replicated, may hold values from 0.1 to 1.9
- enc_qkv: bfloat16 [1024, 3072], replicated, may hold values from -4 to 4
- enc_out: bfloat16 [1024, 1024], replicated, may hold values from -0.1875 to 0.1875
- up_proj: bfloat16 [1024, 4096], P('ctx', 'tp'), may hold values from -0.1875 to 0.1875
- lat_gain: float32 [4096], replicated, may hold values from 0.1 to 1.9
- query_proj: bfloat16 [4096, 2048], P('ctx', 'tp'), may hold values from -4 to 4
- key_proj: bfloat16 [4096, 512], P('ctx', 'tp'), may hold values from -4 to 4
- value_matrix: bfloat16 [4096, 512], P('ctx', 'tp'), may hold values from -0.09375 to 0.09375
- out_proj: bfloat16 [2048, 4096], P('tp', 'ctx'), may hold values from -0.125 to 0.125
- down_proj: bfloat16 [4096, 1024], P('tp', 'ctx'), may hold values from -0.09375 to 0.09375
Outputs:
- byte_states: bfloat16 [8192, 1024], P(('dp', 'ctx', 'tp')), parts along dimension 0
There are 4 independent parts, one for each index of `dp`. A program takes and returns all parts, laid end to end along the dimension named above; an argument that names none is the same for every part. Nothing has to cross between parts.
Inputs may be any that keep to these rules, and one draw needn't show every extreme that they name: `patch_start`: byte 0 begins a patch; every patch spans 1 to 19 bytes; each aligned group of 1024 bytes holds at most 256 patch starts, and some group holds exactly 256.
All inputs are finite; a program needn't handle non-finite values.
Results may differ from a plain program's by a relative error of at most 0.015.
Values may be sent and summed in bfloat16 or wider, within the bound.
No kernel may reach another device: no remote copies, remote signals or barrier semaphores. Data moves between devices by JAX's collectives and lax.ppermute only.
A program may use at most 128 MiB of HBM per device.

v0:
```python
import jax
import jax.numpy as jnp
from jax import lax
from jax.sharding import PartitionSpec as P

BH = 16
HB = 64
HEAD_SIZE = 128
WIN = 512
EPS = 1e-05


def shifted(block, axis, distance):
    devices = range(lax.axis_size(axis))
    route = [(i - distance, i) for i in devices if i - distance in devices]
    return lax.ppermute(block, axis, route)


def rms_scale(values, gain):
    floats = values.astype(jnp.float32)
    return floats * lax.rsqrt(jnp.mean(floats * floats, axis=-1, keepdims=True) + EPS) * gain


def window_attend(query, keys, values, first):
    n_query = query.shape[0]
    n_key = keys.shape[0]
    qh = query.reshape(n_query, BH, HB)
    kh = keys.reshape(n_key, BH, HB)
    vh = values.reshape(n_key, BH, HB)
    scores = jnp.einsum("qhd,khd->hqk", qh, kh, preferred_element_type=jnp.float32) / jnp.sqrt(
        jnp.float32(HB)
    )
    q_pos = first + jnp.arange(n_query, dtype=jnp.int32)
    k_pos = first - (n_key - n_query) + jnp.arange(n_key, dtype=jnp.int32)
    allowed = (
        (k_pos[None, :] <= q_pos[:, None])
        & (k_pos[None, :] > q_pos[:, None] - WIN)
        & (k_pos[None, :] >= 0)
    )
    scores = jnp.where(allowed[None], scores, jnp.float32(-1e30))
    peak = jnp.max(scores, axis=-1, keepdims=True)
    expo = jnp.where(allowed[None], jnp.exp(scores - peak), jnp.float32(0.0))
    total = jnp.sum(expo, axis=-1, keepdims=True)
    mixed = (
        jnp.einsum(
            "hqk,khd->hqd", expo.astype(jnp.bfloat16), vh, preferred_element_type=jnp.float32
        )
        / total
    )
    return jnp.transpose(mixed, (1, 0, 2)).reshape(n_query, BH * HB).astype(jnp.bfloat16)


def local(
    byte_embed,
    patch_start,
    enc_gain,
    enc_qkv,
    enc_out,
    up_proj,
    lat_gain,
    query_proj,
    key_proj,
    value_matrix,
    out_proj,
    down_proj,
):
    nbytes = byte_embed.shape[0]
    width = byte_embed.shape[1]
    n_tp = lax.axis_size("tp")
    n_ctx = lax.axis_size("ctx")
    device = lax.axis_index(("ctx", "tp"))
    group = device // n_tp
    slots = n_tp * nbytes // 4
    normed = rms_scale(byte_embed, enc_gain).astype(jnp.bfloat16)
    qkv = jnp.dot(normed, enc_qkv, preferred_element_type=jnp.float32).astype(jnp.bfloat16)
    query = qkv[:, :width]
    earlier = (qkv[:, width : 2 * width], qkv[:, 2 * width :])
    key_list = [earlier[0]]
    value_list = [earlier[1]]
    for step in range(2):
        earlier = shifted((earlier[0], earlier[1]), ("ctx", "tp"), 1)
        key_list.insert(0, earlier[0])
        value_list.insert(0, earlier[1])
    context = window_attend(
        query,
        jnp.concatenate(key_list, axis=0),
        jnp.concatenate(value_list, axis=0),
        device * nbytes,
    )
    hidden = (
        byte_embed.astype(jnp.float32)
        + jnp.dot(context, enc_out, preferred_element_type=jnp.float32)
    ).astype(jnp.bfloat16)
    local_count = jnp.sum(patch_start)
    all_counts = lax.all_gather(local_count[None], ("ctx", "tp"), axis=0, tiled=True)
    before = jnp.cumsum(all_counts) - all_counts
    offset = before[device] - before[group * n_tp]
    group_counts = jnp.sum(all_counts.reshape(n_ctx, n_tp), axis=1)
    local_slot = jnp.cumsum(patch_start) - 1
    slot = offset + local_slot
    columns = jnp.arange(slots, dtype=jnp.int32)
    onehot = ((slot[:, None] == columns[None, :]) & (local_slot[:, None] >= 0)).astype(jnp.bfloat16)
    part_sum = jnp.dot(onehot.T, hidden, preferred_element_type=jnp.float32)
    part_count = jnp.sum(onehot.astype(jnp.float32), axis=0)
    leading = (local_slot < 0).astype(jnp.bfloat16)
    lead_sum = jnp.dot(leading[None, :], hidden, preferred_element_type=jnp.float32)
    lead_count = jnp.sum(leading.astype(jnp.float32))[None]
    recv_sum, recv_count = shifted((lead_sum, lead_count), ("ctx", "tp"), -1)
    last = offset + local_count - 1
    last_hot = (columns == last).astype(jnp.float32)
    part_sum = part_sum + last_hot[:, None] * recv_sum
    part_count = part_count + last_hot * recv_count
    sums, counts = (
        lax.psum_scatter(
            part_sum.astype(jnp.bfloat16), "tp", scatter_dimension=0, tiled=True
        ).astype(jnp.float32),
        lax.psum_scatter(
            part_count.astype(jnp.bfloat16), "tp", scatter_dimension=0, tiled=True
        ).astype(jnp.float32),
    )
    share = (sums / jnp.maximum(counts, 1.0)[:, None]).astype(jnp.bfloat16)
    pooled = lax.all_gather(share, "tp", axis=0, tiled=True)
    latent_part = jnp.dot(
        pooled,
        lax.all_gather(up_proj, "ctx", axis=0, tiled=True),
        preferred_element_type=jnp.float32,
    ).astype(jnp.bfloat16)
    latent = lax.all_gather(latent_part, "tp", axis=1, tiled=True)
    lnorm = rms_scale(latent, lat_gain).astype(jnp.bfloat16)

    def proj_add(piece):
        return jnp.dot(lnorm, piece, preferred_element_type=jnp.float32)

    q_sum = proj_add(lax.all_gather(query_proj, "ctx", axis=0, tiled=True))
    pieces = (
        lax.all_gather(key_proj, "ctx", axis=0, tiled=True),
        lax.all_gather(value_matrix, "ctx", axis=0, tiled=True),
    )
    k_sum, v_sum = tuple((proj_add(pieces[i]) for i in range(2)))
    q_local = q_sum.astype(jnp.bfloat16)
    k_local = k_sum.astype(jnp.bfloat16)
    v_local = v_sum.astype(jnp.bfloat16)
    heads_local = q_local.shape[1] // HEAD_SIZE
    kv_local = k_local.shape[1] // HEAD_SIZE
    share_count = heads_local // kv_local
    q_grouped = jnp.transpose(
        q_local.reshape(slots, kv_local, share_count, HEAD_SIZE), (1, 2, 0, 3)
    ).reshape(kv_local, share_count * slots, HEAD_SIZE)
    query_rows = group * slots + jnp.tile(jnp.arange(slots, dtype=jnp.int32), share_count)
    scale = 1.0 / jnp.sqrt(jnp.float32(HEAD_SIZE))
    peak = jnp.full((kv_local, share_count * slots), -1e30, jnp.float32)
    k_piece = lax.all_gather(k_local, "ctx", axis=0, tiled=True)
    v_piece = lax.all_gather(v_local, "ctx", axis=0, tiled=True)
    count = k_piece.shape[0]
    k_heads = jnp.transpose(k_piece.reshape(count, kv_local, HEAD_SIZE), (1, 0, 2))
    v_heads = jnp.transpose(v_piece.reshape(count, kv_local, HEAD_SIZE), (1, 0, 2))
    key_rows = jnp.arange(count, dtype=jnp.int32)
    used = key_rows % slots < group_counts[key_rows // slots]
    allowed = used[None, :] & (key_rows[None, :] <= query_rows[:, None])
    scores = (
        jnp.einsum("hqd,hkd->hqk", q_grouped, k_heads, preferred_element_type=jnp.float32) * scale
    )
    scores = jnp.where(allowed[None], scores, jnp.float32(-1e30))
    new_peak = jnp.maximum(peak, jnp.max(scores, axis=-1))
    expo = jnp.where(allowed[None], jnp.exp(scores - new_peak[..., None]), jnp.float32(0.0))
    total = jnp.sum(expo, axis=-1)
    accum = jnp.einsum(
        "hqk,hkd->hqd", expo.astype(jnp.bfloat16), v_heads, preferred_element_type=jnp.float32
    )
    peak, total, accum = (new_peak, total, accum)
    mixed = accum / total[..., None]
    attn = (
        jnp.transpose(mixed.reshape(kv_local, share_count, slots, HEAD_SIZE), (2, 0, 1, 3))
        .reshape(slots, heads_local * HEAD_SIZE)
        .astype(jnp.bfloat16)
    )
    partial_value = jnp.dot(
        attn,
        lax.all_gather(out_proj, "ctx", axis=1, tiled=True),
        preferred_element_type=jnp.float32,
    )
    attn_part = lax.psum_scatter(
        partial_value.astype(jnp.bfloat16), "tp", scatter_dimension=1, tiled=True
    ).astype(jnp.float32)
    latent_out = (latent_part.astype(jnp.float32) + attn_part).astype(jnp.bfloat16)
    down_part = jnp.dot(
        latent_out,
        lax.all_gather(down_proj, "ctx", axis=1, tiled=True),
        preferred_element_type=jnp.float32,
    )
    patch_out = lax.psum(down_part.astype(jnp.bfloat16), "tp")
    trailing = lax.dynamic_slice_in_dim(patch_out, last, 1, 0)
    carried = shifted(trailing, ("ctx", "tp"), 1)
    spread = jnp.dot(onehot, patch_out, preferred_element_type=jnp.float32) + leading.astype(
        jnp.float32
    )[:, None] * carried.astype(jnp.float32)
    return (hidden.astype(jnp.float32) + spread).astype(jnp.bfloat16)


def solution(mesh):
    placed = (
        P(("dp", "ctx", "tp"), None),
        P(("dp", "ctx", "tp")),
        P(),
        P(),
        P(),
        P("ctx", "tp"),
        P(),
        P("ctx", "tp"),
        P("ctx", "tp"),
        P("ctx", "tp"),
        P("tp", "ctx"),
        P("tp", "ctx"),
    )
    return jax.shard_map(
        local, mesh=mesh, in_specs=placed, out_specs=P(("dp", "ctx", "tp"), None), check_vma=False
    )
```

profile of v0, /device:TPU:2, one launch (start us, length us, event | category | flops | bytes accessed | tf_op | source)
XLA Modules:
  0.0 421.7 jit_solution(6950951048192426557)
XLA Ops:
  8.8 4.9 %convolution_convert_fusion.1 = bf16[256,3072]{1,0:T(8,128)(2,1)S(1)} fusion(bf16[1024,3072]{1,0:T(8,128)(2,1)} %param.15, bf16[256,1024]{1,0:T(8,128)(2,1)} %param.12, f32[1024]{0:T(1024)} %param.14, f32[256]{0:T(256)S(1)} %add_rsqrt_fusion.1), kind=kOutput, calls=%fused_computation.15 | convolution fusion | flops 1612447744 | bytes 8393728 | tf_op jit(solution)/shard_map/dot_general | solution.py:75
  19.0 3.5 collective-permute-start.2
  22.5 7.2 %all-reduce = s32[8]{0:T(128)S(1)} all-reduce(s32[8]{0:T(128)S(1)} %dynamic-update-slice), channel_id=1, replica_groups=mesh['ctx'=2,'tp'=4,'dp'=4] {'ctx','tp'}, use_global_device_ids=true, to_apply=%add | all-reduce | flops 8 | bytes 64
  34.9 2.8 collective-permute-start.3
  39.5 6.8 %collective-permute-done.1 = bf16[256,1024]{1,0:T(8,128)(2,1)} collective-permute-done((bf16[256,1024]{1,0:T(8,128)(2,1)}, bf16[256,1024]{1,0:T(8,128)(2,1)}, u32[]{:S(2)}, u32[]{:S(2)}) %collective-permute-start.1) | collective-permute-done | bytes 524320 | tf_op jit(solution)/shard_map/ppermute | solution.py:16
  46.3 2.6 pad_maximum_fusion
  49.0 2.6 copy.27
  54.4 2.7 copy.28
  57.2 8.5 %fusion.67 = (f32[16,256]{1,0:T(8,128)S(1)}, bf16[16,256,768]{2,1,0:T(8,128)(2,1)}) fusion(pred[256,768]{1,0:T(8,128)(4,1)S(1)} %and_and_fusion, bf16[256,16,64]{0,2,1:T(8,128)(2,1)S(1)} %bitcast.72, bf16[768,16,64]{0,2,1:T(8,128)(2,1)} %bitcast.68), kind=kOutput, calls=%fused_computation.103 | convolution fusion | flops 421528320 | bytes 8601600 | tf_op jit(solution)/shard_map/sub | solution.py:42
  65.6 5.3 %fusion.23 = bf16[256,16,64]{0,2,1:T(8,128)(2,1)S(1)} fusion(bf16[768,16,64]{0,2,1:T(8,128)(2,1)} %bitcast.69, bf16[16,256,768]{2,1,0:T(8,128)(2,1)} %get-tuple-element.16, f32[256,16]{0,1:T(8,128)S(1)} %bitcast.82), kind=kOutput, calls=%fused_computation.36 | convolution fusion | flops 403177472 | bytes 8404992 | tf_op jit(solution)/shard_map/hqk,khd->hqd/dot_general | solution.py:45
  77.7 4.5 %collective-permute-start.5 = (f32[1]{0:T(128)}, f32[1]{0:T(128)}, u32[]{:S(2)}, u32[]{:S(2)}) collective-permute-start(f32[1]{0:T(128)} %bitcast.17), channel_id=1, source_target_pairs={{4,0},{8,4},{12,8},{16,12},{20,16},{24,20},{28,24},{5,1},{9,5},{13... | collective-permute-start | bytes 20 | tf_op jit(solution)/shard_map/ppermute | solution.py:16
  84.2 5.8 %all-reduce.1 = bf16[256]{0:T(256)(128)(2,1)S(1)} all-reduce(bf16[256]{0:T(256)(128)(2,1)S(1)} %add_convert_fusion.4), channel_id=3, replica_groups=mesh['ctx'=2,'tp'=4,'dp'=4] {'tp'}, use_global_device_ids=true, to_apply=%region_10.11.clone | all-reduce | flops 256 | bytes 1024
  90.1 9.6 %reduce-scatter.3.cloned.1.call-done = bf16[64,1024]{1,0:T(8,128)(2,1)} async-done(((bf16[256,1024]{1,0:T(8,128)(2,1)}), bf16[64,1024]{1,0:T(8,128)(2,1)}) %reduce-scatter.3.cloned.1.call-update) | async-done | bytes 131088 | tf_op jit(solution)/shard_map/reduce_scatter | solution.py:114
  100.7 6.6 %all_gather.34 = bf16[256,1024]{1,0:T(8,128)(2,1)S(1)} all-gather(bf16[64,1024]{1,0:T(8,128)(2,1)S(1)} %divide_convert_fusion), channel_id=1, replica_groups=mesh['ctx'=2,'tp'=4,'dp'=4] {'tp'}, dimensions={0}, use_global_device_ids=true | all-gather | bytes 655360 | tf_op jit(solution)/shard_map/all_gather | solution.py:122
  107.3 4.4 %all-gather.8.cloned.1.call-done = bf16[1024,1024]{1,0:T(8,128)(2,1)} async-done(((bf16[512,1024]{1,0:T(8,128)(2,1)}), bf16[1024,1024]{1,0:T(8,128)(2,1)}) %all-gather.8.cloned.1.call-update) | async-done | bytes 2097168 | tf_op jit(solution)/shard_map/all_gather | solution.py:125
  111.7 3.1 convolution_convert_fusion.3
  120.5 18.2 %all-gather.10.cloned.1.call-done = bf16[256,4096]{1,0:T(8,128)(2,1)} async-done(((bf16[256,1024]{1,0:T(8,128)(2,1)}), bf16[256,4096]{1,0:T(8,128)(2,1)}) %all-gather.10.cloned.1.call-update) | async-done | bytes 2097168 | tf_op jit(solution)/shard_map/all_gather | solution.py:128
  140.7 55.1 %all-gather.12.cloned.1.call-done = bf16[4096,512]{1,0:T(8,128)(2,1)} async-done(((bf16[2048,512]{1,0:T(8,128)(2,1)}), bf16[4096,512]{1,0:T(8,128)(2,1)}) %all-gather.12.cloned.1.call-update) | async-done | bytes 4194320 | tf_op jit(solution)/shard_map/all_gather | solution.py:134
  195.8 4.1 convolution_convert_fusion.4
  200.0 18.5 %all-gather.14.cloned.1.call-done = bf16[4096,128]{1,0:T(8,128)(2,1)} async-done(((bf16[2048,128]{1,0:T(8,128)(2,1)}), bf16[4096,128]{1,0:T(8,128)(2,1)}) %all-gather.14.cloned.1.call-update) | async-done | bytes 1048592 | tf_op jit(solution)/shard_map/all_gather | solution.py:136
  218.5 2.7 convolution_convert_fusion.6
  221.2 4.9 %all_gather.39 = bf16[512,128]{1,0:T(8,128)(2,1)S(1)} all-gather(bf16[256,128]{1,0:T(8,128)(2,1)S(1)} %convolution_convert_fusion.6), channel_id=1, replica_groups=mesh['ctx'=2,'tp'=4,'dp'=4] {'ctx'}, dimensions={0}, use_global_device_ids=true | all-gather | bytes 196608 | tf_op jit(solution)/shard_map/all_gather | solution.py:152
  226.1 15.1 %all-gather.16.cloned.1.call-done = bf16[4096,128]{1,0:T(8,128)(2,1)} async-done(((bf16[2048,128]{1,0:T(8,128)(2,1)}), bf16[4096,128]{1,0:T(8,128)(2,1)}) %all-gather.16.cloned.1.call-update) | async-done | bytes 1048592 | tf_op jit(solution)/shard_map/all_gather | solution.py:137
  241.2 2.7 convolution_convert_fusion.5
  243.9 4.9 %all_gather.41 = bf16[512,128]{1,0:T(8,128)(2,1)S(1)} all-gather(bf16[256,128]{1,0:T(8,128)(2,1)S(1)} %convolution_convert_fusion.5), channel_id=1, replica_groups=mesh['ctx'=2,'tp'=4,'dp'=4] {'ctx'}, dimensions={0}, use_global_device_ids=true | all-gather | bytes 196608 | tf_op jit(solution)/shard_map/all_gather | solution.py:153
  251.2 48.2 %all-gather.18.cloned.1.call-done = bf16[512,4096]{1,0:T(8,128)(2,1)} async-done(((bf16[512,2048]{1,0:T(8,128)(2,1)}), bf16[512,4096]{1,0:T(8,128)(2,1)}) %all-gather.18.cloned.1.call-update) | async-done | bytes 4194320 | tf_op jit(solution)/shard_map/all_gather | solution.py:179
  299.4 4.8 %convolution_convert_fusion = bf16[256,4096]{1,0:T(8,128)(2,1)} fusion(bf16[256,512]{0,1:T(8,128)(2,1)S(1)} %bitcast.70, bf16[512,4096]{1,0:T(8,128)(2,1)} %all-gather.18.cloned.1.call-done), kind=kOutput, calls=%fused_computation.11 | convolution fusion | flops 1074790400 | bytes 6553600 | tf_op jit(solution)/shard_map/dot_general | solution.py:177
  304.2 29.8 %all-gather.20.cloned.1.call-done = bf16[1024,1024]{1,0:T(8,128)(2,1)} async-done(((bf16[1024,512]{1,0:T(8,128)(2,1)}), bf16[1024,1024]{1,0:T(8,128)(2,1)}) %all-gather.20.cloned.1.call-update) | async-done | bytes 2097168 | tf_op jit(solution)/shard_map/all_gather | solution.py:188
  334.0 34.9 %reduce-scatter.5.cloned.1.call-done = bf16[256,1024]{1,0:T(8,128)(2,1)} async-done(((bf16[256,4096]{1,0:T(8,128)(2,1)}), bf16[256,1024]{1,0:T(8,128)(2,1)}) %reduce-scatter.5.cloned.1.call-update) | async-done | bytes 524304 | tf_op jit(solution)/shard_map/reduce_scatter | solution.py:182
  368.9 3.3 convolution_convert_fusion.2
  372.2 33.6 %all-reduce.4.cloned.1.call-done = bf16[256,1024]{1,0:T(8,128)(2,1)} async-done(((bf16[256,1024]{1,0:T(8,128)(2,1)}), bf16[256,1024]{1,0:T(8,128)(2,1)}) %all-reduce.4.cloned.1.call-update) | async-done | bytes 524304 | tf_op jit(solution)/shard_map/psum | solution.py:191
  408.4 3.9 collective-permute-done.6
  (98 shorter events, 38.9 us)
Async XLA Ops:
  7.4 63.6 %copy-start = (bf16[1024,1024]{1,0:T(8,128)(2,1)S(1)}, bf16[1024,1024]{1,0:T(8,128)(2,1)}, u32[]{:S(2)}) copy-start(bf16[1024,1024]{1,0:T(8,128)(2,1)} %param.16) | copy-start | bytes 6291460
  7.4 92.3 %reduce-scatter.3.cloned.1.call-start = ((), (), s32[]{:S(2)}) async-start(), calls=%async_computation.2 | async-start | bytes 655360 | tf_op jit(solution)/shard_map/reduce_scatter | solution.py:114
  13.6 2.9 copy-start.7
  13.6 3.5 copy-start.4
  14.6 17.9 %collective-permute-start = (bf16[256,1024]{1,0:T(8,128)(2,1)}, bf16[256,1024]{1,0:T(8,128)(2,1)}, u32[]{:S(2)}, u32[]{:S(2)}) collective-permute-start(bf16[256,1024]{1,0:T(8,128)(2,1)} %get-tuple-element.8), channel_id=1, source_target_pairs={{0,4},{4,8},{8,12},{12,16},{16,20},{20,24},{24,28},{1,5},{5,9},{9,... | collective-permute-start | bytes 1572872 | tf_op jit(solution)/shard_map/ppermute | solution.py:16
  19.0 15.9 %collective-permute-start.2 = (bf16[256,1024]{1,0:T(8,128)(2,1)S(1)}, bf16[256,1024]{1,0:T(8,128)(2,1)}, u32[]{:S(2)}, u32[]{:S(2)}) collective-permute-start(bf16[256,1024]{1,0:T(8,128)(2,1)S(1)} %get-tuple-element.9), channel_id=1, source_target_pairs={{0,4},{4,8},{8,12},{12,16},{16,20},{20,24},{24,28},{1,5},{5,9},{9,... | collective-permute-start | bytes 1572872 | tf_op jit(solution)/shard_map/ppermute | solution.py:16
  32.5 13.9 %collective-permute-start.1 = (bf16[256,1024]{1,0:T(8,128)(2,1)}, bf16[256,1024]{1,0:T(8,128)(2,1)}, u32[]{:S(2)}, u32[]{:S(2)}) collective-permute-start(bf16[256,1024]{1,0:T(8,128)(2,1)} %collective-permute-done), channel_id=1, source_target_pairs={{0,4},{4,8},{8,12},{12,16},{16,20},{20,24},{24,28},{1,5},{5,9},{9,... | collective-permute-start | bytes 1572872 | tf_op jit(solution)/shard_map/ppermute | solution.py:16
  34.9 17.1 %collective-permute-start.3 = (bf16[256,1024]{1,0:T(8,128)(2,1)}, bf16[256,1024]{1,0:T(8,128)(2,1)}, u32[]{:S(2)}, u32[]{:S(2)}) collective-permute-start(bf16[256,1024]{1,0:T(8,128)(2,1)} %collective-permute-done.2), channel_id=1, source_target_pairs={{0,4},{4,8},{8,12},{12,16},{16,20},{20,24},{24,28},{1,5},{5,9},{9,... | collective-permute-start | bytes 1572872 | tf_op jit(solution)/shard_map/ppermute | solution.py:16
  54.4 2.7 copy-start.3
  65.6 5.3 %copy-start.1 = (bf16[256,1024]{1,0:T(8,128)(2,1)S(1)}, bf16[256,1024]{1,0:T(8,128)(2,1)}, u32[]{:S(2)}) copy-start(bf16[256,1024]{1,0:T(8,128)(2,1)} %param.12) | copy-start | bytes 1572868
  71.7 10.5 %copy-start.6 = (u32[32]{0:T(128)S(1)}, u32[32]{0:T(128)}, u32[]{:S(2)}) copy-start(u32[32]{0:T(128)} %constant.112) | copy-start | bytes 388
  71.9 3.2 collective-permute-start.4
  76.4 35.3 %all-gather.8.cloned.1.call-start = ((), (), s32[]{:S(2)}) async-start(), calls=%async_computation.3 | async-start | bytes 3145728 | tf_op jit(solution)/shard_map/all_gather | solution.py:125
  76.9 61.7 %all-gather.10.cloned.1.call-start = ((), (), s32[]{:S(2)}) async-start(), calls=%async_computation.4 | async-start | bytes 2621440 | tf_op jit(solution)/shard_map/all_gather | solution.py:128
  77.7 5.9 %collective-permute-start.5 = (f32[1]{0:T(128)}, f32[1]{0:T(128)}, u32[]{:S(2)}, u32[]{:S(2)}) collective-permute-start(f32[1]{0:T(128)} %bitcast.17), channel_id=1, source_target_pairs={{4,0},{8,4},{12,8},{16,12},{20,16},{24,20},{28,24},{5,1},{9,5},{13... | collective-permute-start | bytes 20 | tf_op jit(solution)/shard_map/ppermute | solution.py:16
  114.8 81.0 %all-gather.12.cloned.1.call-start = ((), (), s32[]{:S(2)}) async-start(), calls=%async_computation.5 | async-start | bytes 6291456 | tf_op jit(solution)/shard_map/all_gather | solution.py:134
  115.5 103.0 %all-gather.14.cloned.1.call-start = ((), (), s32[]{:S(2)}) async-start(), calls=%async_computation.6 | async-start | bytes 1572864 | tf_op jit(solution)/shard_map/all_gather | solution.py:136
  116.1 125.1 %all-gather.16.cloned.1.call-start = ((), (), s32[]{:S(2)}) async-start(), calls=%async_computation.7 | async-start | bytes 1572864 | tf_op jit(solution)/shard_map/all_gather | solution.py:137
  116.7 182.7 %all-gather.18.cloned.1.call-start = ((), (), s32[]{:S(2)}) async-start(), calls=%async_computation.8 | async-start | bytes 6291456 | tf_op jit(solution)/shard_map/all_gather | solution.py:179
  117.3 78.5 %copy-start.5 = (f32[4096]{0:T(1024)S(1)}, f32[4096]{0:T(1024)}, u32[]{:S(2)}) copy-start(f32[4096]{0:T(1024)} %param.18) | copy-start | bytes 49156
  117.3 216.8 %all-gather.20.cloned.1.call-start = ((), (), s32[]{:S(2)}) async-start(), calls=%async_computation.10 | async-start | bytes 3145728 | tf_op jit(solution)/shard_map/all_gather | solution.py:188
  118.0 250.9 %reduce-scatter.5.cloned.1.call-start = ((), (), s32[]{:S(2)}) async-start(), calls=%async_computation.9 | async-start | bytes 2621440 | tf_op jit(solution)/shard_map/reduce_scatter | solution.py:182
  304.2 64.7 %copy-start.2 = (bf16[256,1024]{1,0:T(8,128)(2,1)S(1)}, bf16[256,1024]{1,0:T(8,128)(2,1)}, u32[]{:S(2)}) copy-start(bf16[256,1024]{1,0:T(8,128)(2,1)} %convolution_convert_fusion.3) | copy-start | bytes 1572868
  304.2 101.6 %all-reduce.4.cloned.1.call-start = ((), (), s32[]{:S(2)}) async-start(), calls=%async_computation.11 | async-start | bytes 1048576 | tf_op jit(solution)/shard_map/psum | solution.py:191
  406.5 5.8 %collective-permute-start.6 = (bf16[1,1024]{1,0:T(2,128)(2,1)S(1)}, bf16[1,1024]{1,0:T(2,128)(2,1)S(1)}, u32[]{:S(2)}, u32[]{:S(2)}) collective-permute-start(bf16[1,1024]{1,0:T(2,128)(2,1)S(1)} %constant_dynamic-slice_fusion), channel_id=1, source_target_pairs={{0,4},{4,8},{8,12},{12,16},{16,20},{20,24},{24,28},{1,5},{5,9},{9,... | collective-permute-start | bytes 6152 | tf_op jit(solution)/shard_map/ppermute | solution.py:16
Sparse Core Ops, SparseCore 0:
  76.5 23.1 reduce-scatter.2
  114.9 23.6 all-gather.9
  140.2 55.5 all-gather.11
  197.2 21.2 all-gather.13
  219.9 21.2 all-gather.15
  242.6 56.7 all-gather.17
  300.9 33.0 all-gather.19
  336.6 32.2 reduce-scatter.4
  372.3 33.4 all-reduce.3
Sparse Core Ops, SparseCore 1:
  78.4 33.2 all-gather.7
where the time goes:
time: 422 us
  waiting for transfers between devices  283 us (67%)
  matrix products  45.1 us (11%)
  blocking collectives  29.4 us (7%)
  starting transfers between devices  19.5 us (5%)
  between operations  17.4 us (4%)
  other arithmetic  14.7 us (3%)
  local copies, waits for them, and re-layouts  12.3 us (3%)
    all_gather x1, waiting for transfers between devices, local(): q_sum = proj_add(lax.all_gather(query_proj, 'ctx', axis=0, tiled=True))  55.1 us
    all_gather x1, waiting for transfers between devices, local(): lax.all_gather(out_proj, 'ctx', axis=1, tiled=True)  48.2 us
    reduce_scatter x1, waiting for transfers between devices, local(): lax.psum_scatter(partial_value.astype(jnp.bfloat16), 'tp', scatter_dimens...  34.9 us
    psum x1, waiting for transfers between devices, local(): patch_out = lax.psum(down_part.astype(jnp.bfloat16), 'tp')  33.6 us
    all_gather x1, waiting for transfers between devices, local(): lax.all_gather(down_proj, 'ctx', axis=1, tiled=True)  29.8 us
    ppermute x7, starting transfers between devices, shifted(): return lax.ppermute(block, axis, route)  18.9 us
    all_gather x1, waiting for transfers between devices, local(): lax.all_gather(key_proj, 'ctx', axis=0, tiled=True)  18.5 us
    all_gather x1, waiting for transfers between devices, local(): latent = lax.all_gather(latent_part, 'tp', axis=1, tiled=True)  18.2 us
  transfers between devices with their start and end apart: 17, of which 14 were waited for; matrix products, arithmetic and copies ran while one was open for 8% of the time, Pallas kernels for 0%

commit v1 on v0

--- a/solution.py
+++ b/solution.py
@@ -8,6 +8,16 @@
 HEAD_SIZE = 128
 WIN = 512
 EPS = 1e-05
+
+
+def _mark_patches(field_in, in_array):
+    return jnp.split(
+        lax.all_gather(
+            jnp.concatenate([in_array, field_in], axis=1), axis_name="ctx", axis=0, tiled=True
+        ),
+        [in_array.shape[1]],
+        axis=1,
+    )
 
 
 def shifted(block, axis, distance):
@@ -149,8 +159,7 @@
     query_rows = group * slots + jnp.tile(jnp.arange(slots, dtype=jnp.int32), share_count)
     scale = 1.0 / jnp.sqrt(jnp.float32(HEAD_SIZE))
     peak = jnp.full((kv_local, share_count * slots), -1e30, jnp.float32)
-    k_piece = lax.all_gather(k_local, "ctx", axis=0, tiled=True)
-    v_piece = lax.all_gather(v_local, "ctx", axis=0, tiled=True)
+    k_piece, v_piece = _mark_patches(v_local, in_array=k_local)
     count = k_piece.shape[0]
     k_heads = jnp.transpose(k_piece.reshape(count, kv_local, HEAD_SIZE), (1, 0, 2))
     v_heads = jnp.transpose(v_piece.reshape(count, kv_local, HEAD_SIZE), (1, 0, 2))

time: 422 us -> 422 us (level)
    all_gather x1, waiting for transfers between devices: 15.1 us -> 19.8 us  [local(): lax.all_gather(value_matrix, 'ctx', axis=0, tiled=True)]
    all_gather x2 -> x1, blocking collectives: 9.87 us -> 5.92 us  [_mark_patches(): lax.all_gather(jnp.concatenate([in_array, field_in], axis=1), axis_name='...]
where the time goes in v1:
time: 422 us
  waiting for transfers between devices  287 us (68%)
  matrix products  45.5 us (11%)
  blocking collectives  25.5 us (6%)
  starting transfers between devices  19.5 us (5%)
  between operations  17.4 us (4%)
  other arithmetic  14.7 us (3%)
  local copies, waits for them, and re-layouts  12.3 us (3%)
    all_gather x1, waiting for transfers between devices, local(): q_sum = proj_add(lax.all_gather(query_proj, 'ctx', axis=0, tiled=True))  55.1 us
    all_gather x1, waiting for transfers between devices, local(): lax.all_gather(out_proj, 'ctx', axis=1, tiled=True)  46.9 us
    reduce_scatter x1, waiting for transfers between devices, local(): lax.psum_scatter(partial_value.astype(jnp.bfloat16), 'tp', scatter_dimens...  34.9 us
    psum x1, waiting for transfers between devices, local(): patch_out = lax.psum(down_part.astype(jnp.bfloat16), 'tp')  33.6 us
    all_gather x1, waiting for transfers between devices, local(): lax.all_gather(down_proj, 'ctx', axis=1, tiled=True)  29.8 us
    all_gather x1, waiting for transfers between devices, local(): lax.all_gather(value_matrix, 'ctx', axis=0, tiled=True)  19.8 us
    ppermute x7, starting transfers between devices, shifted(): return lax.ppermute(block, axis, route)  18.9 us
    all_gather x1, waiting for transfers between devices, local(): lax.all_gather(key_proj, 'ctx', axis=0, tiled=True)  18.6 us
  transfers between devices with their start and end apart: 17, of which 14 were waited for; matrix products, arithmetic and copies ran while one was open for 8% of the time, Pallas kernels for 0%

profile of v1, /device:TPU:2, one launch (start us, length us, event | category | flops | bytes accessed | tf_op | source)
XLA Modules:
  0.0 421.7 jit_solution(5062676175057190418)
XLA Ops:
  8.8 4.9 %convolution_convert_fusion.1 = bf16[256,3072]{1,0:T(8,128)(2,1)S(1)} fusion(bf16[1024,3072]{1,0:T(8,128)(2,1)} %param.15, bf16[256,1024]{1,0:T(8,128)(2,1)} %param.12, f32[1024]{0:T(1024)} %param.14, f32[256]{0:T(256)S(1)} %add_rsqrt_fusion.1), kind=kOutput, calls=%fused_computation.15 | convolution fusion | flops 1612447744 | bytes 8393728 | tf_op jit(solution)/shard_map/dot_general | solution.py:85
  19.0 3.5 collective-permute-start.2
  22.5 7.2 %all-reduce = s32[8]{0:T(128)S(1)} all-reduce(s32[8]{0:T(128)S(1)} %dynamic-update-slice), channel_id=1, replica_groups=mesh['ctx'=2,'tp'=4,'dp'=4] {'ctx','tp'}, use_global_device_ids=true, to_apply=%add | all-reduce | flops 8 | bytes 64
  34.9 2.8 collective-permute-start.3
  39.5 6.8 %collective-permute-done.1 = bf16[256,1024]{1,0:T(8,128)(2,1)} collective-permute-done((bf16[256,1024]{1,0:T(8,128)(2,1)}, bf16[256,1024]{1,0:T(8,128)(2,1)}, u32[]{:S(2)}, u32[]{:S(2)}) %collective-permute-start.1) | collective-permute-done | bytes 524320 | tf_op jit(solution)/shard_map/ppermute | solution.py:26
  46.3 2.6 pad_maximum_fusion
  49.0 2.6 copy.27
  51.9 2.5 pad_maximum_fusion.1
  54.4 2.7 copy.28
  57.2 8.5 %fusion.69 = (f32[16,256]{1,0:T(8,128)S(1)}, bf16[16,256,768]{2,1,0:T(8,128)(2,1)}) fusion(pred[256,768]{1,0:T(8,128)(4,1)S(1)} %and_and_fusion, bf16[256,16,64]{0,2,1:T(8,128)(2,1)S(1)} %bitcast.70, bf16[768,16,64]{0,2,1:T(8,128)(2,1)} %bitcast.66), kind=kOutput, calls=%fused_computation.106 | convolution fusion | flops 421528320 | bytes 8601600 | tf_op jit(solution)/shard_map/sub | solution.py:52
  65.6 5.3 %fusion.23 = bf16[256,16,64]{0,2,1:T(8,128)(2,1)S(1)} fusion(bf16[768,16,64]{0,2,1:T(8,128)(2,1)} %bitcast.67, bf16[16,256,768]{2,1,0:T(8,128)(2,1)} %get-tuple-element.16, f32[256,16]{0,1:T(8,128)S(1)} %bitcast.80), kind=kOutput, calls=%fused_computation.36 | convolution fusion | flops 403177472 | bytes 8404992 | tf_op jit(solution)/shard_map/hqk,khd->hqd/dot_general | solution.py:55
  77.7 4.5 %collective-permute-start.5 = (f32[1]{0:T(128)}, f32[1]{0:T(128)}, u32[]{:S(2)}, u32[]{:S(2)}) collective-permute-start(f32[1]{0:T(128)} %bitcast.17), channel_id=1, source_target_pairs={{4,0},{8,4},{12,8},{16,12},{20,16},{24,20},{28,24},{5,1},{9,5},{13... | collective-permute-start | bytes 20 | tf_op jit(solution)/shard_map/ppermute | solution.py:26
  84.2 5.8 %all-reduce.1 = bf16[256]{0:T(256)(128)(2,1)S(1)} all-reduce(bf16[256]{0:T(256)(128)(2,1)S(1)} %add_convert_fusion.4), channel_id=3, replica_groups=mesh['ctx'=2,'tp'=4,'dp'=4] {'tp'}, use_global_device_ids=true, to_apply=%region_10.11.clone | all-reduce | flops 256 | bytes 1024
  90.1 9.6 %reduce-scatter.3.cloned.1.call-done = bf16[64,1024]{1,0:T(8,128)(2,1)} async-done(((bf16[256,1024]{1,0:T(8,128)(2,1)}), bf16[64,1024]{1,0:T(8,128)(2,1)}) %reduce-scatter.3.cloned.1.call-update) | async-done | bytes 131088 | tf_op jit(solution)/shard_map/reduce_scatter | solution.py:124
  100.7 6.6 %all_gather.31 = bf16[256,1024]{1,0:T(8,128)(2,1)S(1)} all-gather(bf16[64,1024]{1,0:T(8,128)(2,1)S(1)} %divide_convert_fusion), channel_id=1, replica_groups=mesh['ctx'=2,'tp'=4,'dp'=4] {'tp'}, dimensions={0}, use_global_device_ids=true | all-gather | bytes 655360 | tf_op jit(solution)/shard_map/all_gather | solution.py:132
  107.3 4.4 %all-gather.8.cloned.1.call-done = bf16[1024,1024]{1,0:T(8,128)(2,1)} async-done(((bf16[512,1024]{1,0:T(8,128)(2,1)}), bf16[1024,1024]{1,0:T(8,128)(2,1)}) %all-gather.8.cloned.1.call-update) | async-done | bytes 2097168 | tf_op jit(solution)/shard_map/all_gather | solution.py:135
  111.7 3.1 convolution_convert_fusion.3
  120.5 18.2 %all-gather.10.cloned.1.call-done = bf16[256,4096]{1,0:T(8,128)(2,1)} async-done(((bf16[256,1024]{1,0:T(8,128)(2,1)}), bf16[256,4096]{1,0:T(8,128)(2,1)}) %all-gather.10.cloned.1.call-update) | async-done | bytes 2097168 | tf_op jit(solution)/shard_map/all_gather | solution.py:138
  140.7 55.1 %all-gather.12.cloned.1.call-done = bf16[4096,512]{1,0:T(8,128)(2,1)} async-done(((bf16[2048,512]{1,0:T(8,128)(2,1)}), bf16[4096,512]{1,0:T(8,128)(2,1)}) %all-gather.12.cloned.1.call-update) | async-done | bytes 4194320 | tf_op jit(solution)/shard_map/all_gather | solution.py:144
  195.8 4.1 convolution_convert_fusion.4
  199.9 18.6 %all-gather.14.cloned.1.call-done = bf16[4096,128]{1,0:T(8,128)(2,1)} async-done(((bf16[2048,128]{1,0:T(8,128)(2,1)}), bf16[4096,128]{1,0:T(8,128)(2,1)}) %all-gather.14.cloned.1.call-update) | async-done | bytes 1048592 | tf_op jit(solution)/shard_map/all_gather | solution.py:146
  218.5 2.8 convolution_convert_fusion.6
  221.5 19.8 %all-gather.16.cloned.1.call-done = bf16[4096,128]{1,0:T(8,128)(2,1)} async-done(((bf16[2048,128]{1,0:T(8,128)(2,1)}), bf16[4096,128]{1,0:T(8,128)(2,1)}) %all-gather.16.cloned.1.call-update) | async-done | bytes 1048592 | tf_op jit(solution)/shard_map/all_gather | solution.py:147
  241.2 2.8 convolution_convert_fusion.5
  244.1 5.9 %all_gather.37 = bf16[512,256]{0,1:T(8,128)(2,1)S(1)} all-gather(bf16[256,256]{0,1:T(8,128)(2,1)S(1)} %pad_maximum_fusion.2), channel_id=1, replica_groups=mesh['ctx'=2,'tp'=4,'dp'=4] {'ctx'}, dimensions={0}, use_global_device_ids=true | all-gather | bytes 393216 | tf_op jit(solution)/shard_map/all_gather | solution.py:15
  252.4 46.9 %all-gather.18.cloned.1.call-done = bf16[512,4096]{1,0:T(8,128)(2,1)} async-done(((bf16[512,2048]{1,0:T(8,128)(2,1)}), bf16[512,4096]{1,0:T(8,128)(2,1)}) %all-gather.18.cloned.1.call-update) | async-done | bytes 4194320 | tf_op jit(solution)/shard_map/all_gather | solution.py:188
  299.4 4.8 %convolution_convert_fusion = bf16[256,4096]{1,0:T(8,128)(2,1)} fusion(bf16[256,512]{0,1:T(8,128)(2,1)S(1)} %bitcast.68, bf16[512,4096]{1,0:T(8,128)(2,1)} %all-gather.18.cloned.1.call-done), kind=kOutput, calls=%fused_computation.11 | convolution fusion | flops 1074790400 | bytes 6553600 | tf_op jit(solution)/shard_map/dot_general | solution.py:186
  304.2 29.8 %all-gather.20.cloned.1.call-done = bf16[1024,1024]{1,0:T(8,128)(2,1)} async-done(((bf16[1024,512]{1,0:T(8,128)(2,1)}), bf16[1024,1024]{1,0:T(8,128)(2,1)}) %all-gather.20.cloned.1.call-update) | async-done | bytes 2097168 | tf_op jit(solution)/shard_map/all_gather | solution.py:197
  334.0 34.9 %reduce-scatter.5.cloned.1.call-done = bf16[256,1024]{1,0:T(8,128)(2,1)} async-done(((bf16[256,4096]{1,0:T(8,128)(2,1)}), bf16[256,1024]{1,0:T(8,128)(2,1)}) %reduce-scatter.5.cloned.1.call-update) | async-done | bytes 524304 | tf_op jit(solution)/shard_map/reduce_scatter | solution.py:191
  368.9 3.3 convolution_convert_fusion.2
  372.2 33.6 %all-reduce.4.cloned.1.call-done = bf16[256,1024]{1,0:T(8,128)(2,1)} async-done(((bf16[256,1024]{1,0:T(8,128)(2,1)}), bf16[256,1024]{1,0:T(8,128)(2,1)}) %all-reduce.4.cloned.1.call-update) | async-done | bytes 524304 | tf_op jit(solution)/shard_map/psum | solution.py:200
  408.4 3.9 collective-permute-done.6
  (98 shorter events, 36.5 us)
Async XLA Ops:
  7.4 63.6 %copy-start = (bf16[1024,1024]{1,0:T(8,128)(2,1)S(1)}, bf16[1024,1024]{1,0:T(8,128)(2,1)}, u32[]{:S(2)}) copy-start(bf16[1024,1024]{1,0:T(8,128)(2,1)} %param.16) | copy-start | bytes 6291460
  7.4 92.3 %reduce-scatter.3.cloned.1.call-start = ((), (), s32[]{:S(2)}) async-start(), calls=%async_computation.2 | async-start | bytes 655360 | tf_op jit(solution)/shard_map/reduce_scatter | solution.py:124
  13.6 2.9 copy-start.7
  13.6 3.5 copy-start.4
  14.6 17.9 %collective-permute-start = (bf16[256,1024]{1,0:T(8,128)(2,1)}, bf16[256,1024]{1,0:T(8,128)(2,1)}, u32[]{:S(2)}, u32[]{:S(2)}) collective-permute-start(bf16[256,1024]{1,0:T(8,128)(2,1)} %get-tuple-element.8), channel_id=1, source_target_pairs={{0,4},{4,8},{8,12},{12,16},{16,20},{20,24},{24,28},{1,5},{5,9},{9,... | collective-permute-start | bytes 1572872 | tf_op jit(solution)/shard_map/ppermute | solution.py:26
  19.0 15.9 %collective-permute-start.2 = (bf16[256,1024]{1,0:T(8,128)(2,1)S(1)}, bf16[256,1024]{1,0:T(8,128)(2,1)}, u32[]{:S(2)}, u32[]{:S(2)}) collective-permute-start(bf16[256,1024]{1,0:T(8,128)(2,1)S(1)} %get-tuple-element.9), channel_id=1, source_target_pairs={{0,4},{4,8},{8,12},{12,16},{16,20},{20,24},{24,28},{1,5},{5,9},{9,... | collective-permute-start | bytes 1572872 | tf_op jit(solution)/shard_map/ppermute | solution.py:26
  32.5 13.9 %collective-permute-start.1 = (bf16[256,1024]{1,0:T(8,128)(2,1)}, bf16[256,1024]{1,0:T(8,128)(2,1)}, u32[]{:S(2)}, u32[]{:S(2)}) collective-permute-start(bf16[256,1024]{1,0:T(8,128)(2,1)} %collective-permute-done), channel_id=1, source_target_pairs={{0,4},{4,8},{8,12},{12,16},{16,20},{20,24},{24,28},{1,5},{5,9},{9,... | collective-permute-start | bytes 1572872 | tf_op jit(solution)/shard_map/ppermute | solution.py:26
  34.9 17.1 %collective-permute-start.3 = (bf16[256,1024]{1,0:T(8,128)(2,1)}, bf16[256,1024]{1,0:T(8,128)(2,1)}, u32[]{:S(2)}, u32[]{:S(2)}) collective-permute-start(bf16[256,1024]{1,0:T(8,128)(2,1)} %collective-permute-done.2), channel_id=1, source_target_pairs={{0,4},{4,8},{8,12},{12,16},{16,20},{20,24},{24,28},{1,5},{5,9},{9,... | collective-permute-start | bytes 1572872 | tf_op jit(solution)/shard_map/ppermute | solution.py:26
  54.4 2.7 copy-start.3
  65.6 5.3 %copy-start.1 = (bf16[256,1024]{1,0:T(8,128)(2,1)S(1)}, bf16[256,1024]{1,0:T(8,128)(2,1)}, u32[]{:S(2)}) copy-start(bf16[256,1024]{1,0:T(8,128)(2,1)} %param.12) | copy-start | bytes 1572868
  71.7 10.5 %copy-start.6 = (u32[32]{0:T(128)S(1)}, u32[32]{0:T(128)}, u32[]{:S(2)}) copy-start(u32[32]{0:T(128)} %constant.112) | copy-start | bytes 388
  71.9 3.2 collective-permute-start.4
  76.4 35.3 %all-gather.8.cloned.1.call-start = ((), (), s32[]{:S(2)}) async-start(), calls=%async_computation.3 | async-start | bytes 3145728 | tf_op jit(solution)/shard_map/all_gather | solution.py:135
  76.9 61.7 %all-gather.10.cloned.1.call-start = ((), (), s32[]{:S(2)}) async-start(), calls=%async_computation.4 | async-start | bytes 2621440 | tf_op jit(solution)/shard_map/all_gather | solution.py:138
  77.7 5.9 %collective-permute-start.5 = (f32[1]{0:T(128)}, f32[1]{0:T(128)}, u32[]{:S(2)}, u32[]{:S(2)}) collective-permute-start(f32[1]{0:T(128)} %bitcast.17), channel_id=1, source_target_pairs={{4,0},{8,4},{12,8},{16,12},{20,16},{24,20},{28,24},{5,1},{9,5},{13... | collective-permute-start | bytes 20 | tf_op jit(solution)/shard_map/ppermute | solution.py:26
  114.8 81.0 %all-gather.12.cloned.1.call-start = ((), (), s32[]{:S(2)}) async-start(), calls=%async_computation.5 | async-start | bytes 6291456 | tf_op jit(solution)/shard_map/all_gather | solution.py:144
  115.5 103.0 %all-gather.14.cloned.1.call-start = ((), (), s32[]{:S(2)}) async-start(), calls=%async_computation.6 | async-start | bytes 1572864 | tf_op jit(solution)/shard_map/all_gather | solution.py:146
  116.1 125.1 %all-gather.16.cloned.1.call-start = ((), (), s32[]{:S(2)}) async-start(), calls=%async_computation.7 | async-start | bytes 1572864 | tf_op jit(solution)/shard_map/all_gather | solution.py:147
  116.7 182.7 %all-gather.18.cloned.1.call-start = ((), (), s32[]{:S(2)}) async-start(), calls=%async_computation.8 | async-start | bytes 6291456 | tf_op jit(solution)/shard_map/all_gather | solution.py:188
  117.3 78.5 %copy-start.5 = (f32[4096]{0:T(1024)S(1)}, f32[4096]{0:T(1024)}, u32[]{:S(2)}) copy-start(f32[4096]{0:T(1024)} %param.18) | copy-start | bytes 49156
  117.3 216.8 %all-gather.20.cloned.1.call-start = ((), (), s32[]{:S(2)}) async-start(), calls=%async_computation.10 | async-start | bytes 3145728 | tf_op jit(solution)/shard_map/all_gather | solution.py:197
  118.0 250.9 %reduce-scatter.5.cloned.1.call-start = ((), (), s32[]{:S(2)}) async-start(), calls=%async_computation.9 | async-start | bytes 2621440 | tf_op jit(solution)/shard_map/reduce_scatter | solution.py:191
  304.2 64.7 %copy-start.2 = (bf16[256,1024]{1,0:T(8,128)(2,1)S(1)}, bf16[256,1024]{1,0:T(8,128)(2,1)}, u32[]{:S(2)}) copy-start(bf16[256,1024]{1,0:T(8,128)(2,1)} %convolution_convert_fusion.3) | copy-start | bytes 1572868
  304.2 101.6 %all-reduce.4.cloned.1.call-start = ((), (), s32[]{:S(2)}) async-start(), calls=%async_computation.11 | async-start | bytes 1048576 | tf_op jit(solution)/shard_map/psum | solution.py:200
  406.5 5.8 %collective-permute-start.6 = (bf16[1,1024]{1,0:T(2,128)(2,1)S(1)}, bf16[1,1024]{1,0:T(2,128)(2,1)S(1)}, u32[]{:S(2)}, u32[]{:S(2)}) collective-permute-start(bf16[1,1024]{1,0:T(2,128)(2,1)S(1)} %constant_dynamic-slice_fusion), channel_id=1, source_target_pairs={{0,4},{4,8},{8,12},{12,16},{16,20},{20,24},{24,28},{1,5},{5,9},{9,... | collective-permute-start | bytes 6152 | tf_op jit(solution)/shard_map/ppermute | solution.py:26
Sparse Core Ops, SparseCore 0:
  76.5 23.1 reduce-scatter.2
  114.9 23.6 all-gather.9
  140.2 55.5 all-gather.11
  197.2 21.2 all-gather.13
  219.9 21.2 all-gather.15
  242.6 56.7 all-gather.17
  300.9 33.0 all-gather.19
  336.6 32.2 reduce-scatter.4
  372.3 33.4 all-reduce.3
Sparse Core Ops, SparseCore 1:
  78.4 33.2 all-gather.7
